TPU v7x, 32 devices: a whole 2x2x4 slice. The times are simulated.
32 devices in a mesh: replica: 4 (over y, core), table: 8 (over z, x).
Axes of the slice: x: 2, y: 2, z: 4, core: 2. Of those that a mesh axis runs over, the one named last changes fastest.
Arguments:
- cache: float32 [768, 16384], P('table', 'replica'), may hold values from -6 to 6
- accum: float32 [768, 16384], P('table', 'replica'), may hold values from 0.5 to 8
- row_ids: int32 [4, 8, 128], P('replica'), may hold values from 0 to 4095
- lengths: int32 [4, 8], P('replica'), may hold values from 1 to 128, 614 in all within a row
- seq_slot: int32 [4, 8], P('replica'), may hold values from 0 to 7, each once within a row
- block_mask: int32 [4, 8, 2, 2], P('replica'), may hold values 0 or 1
- cotangent: bfloat16 [4, 1024, 768], P('replica', 'table'), may hold values from -6 to 6
- w_uqkv: bfloat16 [768, 3072], P('replica'), may hold values from -0.21875 to 0.21875
- w_out: bfloat16 [768, 768], P('replica'), may hold values from -0.21875 to 0.21875
- w2_accum: float32 [768, 768], P('replica', 'table'), may hold values from 81.92 to 8192
Outputs:
- cache_new: float32 [768, 16384], P('table', 'replica')
- accum_new: float32 [768, 16384], P('table', 'replica')
- w2_step: float32 [768, 768], P('replica', 'table')
Inputs may be any that keep to these rules, and one draw needn't show every extreme that they name: `lengths`: in every replica group some sequence has length 128. `seq_slot`: each row names every slot once.
All inputs are finite; a program needn't handle non-finite values. No bound on the sum of `block_mask` on one device may be relied on, other than what follows from the above.
Results may differ from a plain program's by a relative error of at most 0.012.
Values may be sent and summed in bfloat16 or wider, within the bound.
A program may use at most 64 MiB of HBM per device.

v0:
```python
from functools import partial
import jax
import jax.numpy as jnp
from jax import lax
from jax.sharding import PartitionSpec as P

D = 768
HEADS = 12
HEAD_DIM = 64
SEQ_DEV = 1
SEQ_LEN = 128
CAP = 128
EPS_NORM = 1e-05
EPS_ATTN = 1e-06
STEP_SIZE = 0.5


def normalize(row_data):
    centred = row_data - jnp.mean(row_data, axis=-1, keepdims=True)
    variance = jnp.mean(centred * centred, axis=-1, keepdims=True)
    return centred / jnp.sqrt(variance + EPS_NORM)


def pattern_mask(lengths_at, blocks_at, seq_len):
    block_count = blocks_at.shape[-1]
    block_width = seq_len // block_count
    places = jnp.arange(seq_len, dtype=jnp.int32)
    block_of = places // block_width
    same_block = block_of[:, None] == block_of[None, :]
    chosen = jnp.repeat(jnp.repeat(blocks_at, block_width, axis=1), block_width, axis=2) > 0
    chosen = chosen | same_block[None]
    causal = places[None, :] <= places[:, None]
    inside = places[None, :] < lengths_at[:, None]
    allowed = chosen & causal[None] & inside[:, :, None] & inside[:, None, :]
    return (allowed.astype(jnp.float32), inside)


def attention_branch(hidden_pre, allowed):
    slot_count = allowed.shape[0]
    seq_len = allowed.shape[1]
    projected = jax.nn.silu(hidden_pre).astype(jnp.bfloat16)
    gate_u = projected[:, :D]
    queries = projected[:, D : 2 * D].reshape(slot_count, seq_len, HEADS, HEAD_DIM)
    key_rows = projected[:, 2 * D : 3 * D].reshape(slot_count, seq_len, HEADS, HEAD_DIM)
    value_rows = projected[:, 3 * D :].reshape(slot_count, seq_len, HEADS, HEAD_DIM)
    scores = jnp.einsum(
        "sihd,sjhd->shij", queries, key_rows, preferred_element_type=jnp.float32
    ) * HEAD_DIM ** (-0.5)
    weights = (jax.nn.silu(scores) * allowed[:, None]).astype(jnp.bfloat16)
    attended = jnp.einsum(
        "shij,sjhd->sihd", weights, value_rows, preferred_element_type=jnp.float32
    )
    attended = attended.reshape(slot_count * seq_len, D)
    centred_att = attended - jnp.mean(attended, axis=-1, keepdims=True)
    inverse_dev = 1.0 / jnp.sqrt(
        jnp.mean(centred_att * centred_att, axis=-1, keepdims=True) + EPS_ATTN
    )
    return centred_att * inverse_dev * gate_u.astype(jnp.float32)


def body(cache, accum, row_ids, lengths, seq_slot, block_mask, cotangent, w_uqkv, w_out, w2_accum):
    tables = lax.axis_size("table")
    table_index = lax.axis_index("table")
    columns = cache.shape[0]
    seq_count = seq_slot.shape[1]
    sequence_ids = jnp.arange(seq_count, dtype=jnp.int32)
    matches = (seq_slot[0][:, None] == sequence_ids[None, :]).astype(jnp.int32)
    seq_at = jnp.sum(sequence_ids[:, None] * matches, axis=0)
    lengths_at = jnp.sum(lengths[0][:, None] * matches, axis=0)
    slot_ids = row_ids[0][seq_at].reshape(-1)
    own_first = table_index * SEQ_DEV
    own_lengths = lax.dynamic_slice_in_dim(lengths_at, own_first, SEQ_DEV, 0)
    own_blocks = lax.dynamic_slice_in_dim(block_mask[0][seq_at], own_first, SEQ_DEV, 0)
    allowed, inside = pattern_mask(own_lengths, own_blocks, SEQ_LEN)
    picked = jnp.take(cache, slot_ids, axis=1).astype(jnp.bfloat16).reshape(columns, tables, CAP)
    arrived = lax.all_to_all(picked, "table", split_axis=1, concat_axis=0, tiled=True)
    embedded = arrived.reshape(D, CAP).T
    row_float = embedded.astype(jnp.float32)
    normed = normalize(row_float).astype(jnp.bfloat16)
    full_uqkv = lax.all_gather(w_uqkv, "replica", axis=0, tiled=True)
    hidden_pre = jnp.dot(normed, full_uqkv, preferred_element_type=jnp.float32)
    live_cot = cotangent[0] * inside.reshape(-1)[:, None].astype(jnp.bfloat16)
    d_gated = lax.dot_general(
        live_cot,
        lax.all_gather(w_out, "replica", axis=0, tiled=True),
        (((1,), (1,)), ((), ())),
        preferred_element_type=jnp.float32,
    )
    gated_raw, branch_vjp = jax.vjp(partial(attention_branch, allowed=allowed), hidden_pre)
    gated = gated_raw.astype(jnp.bfloat16)
    d_hidden = branch_vjp(d_gated)[0].astype(jnp.bfloat16)
    d_normed = lax.dot_general(
        d_hidden, full_uqkv, (((1,), (1,)), ((), ())), preferred_element_type=jnp.float32
    )
    _, norm_vjp = jax.vjp(normalize, row_float)
    row_grad = live_cot.astype(jnp.float32) + norm_vjp(d_normed)[0]
    sending = row_grad.T.reshape(tables, columns, CAP)
    returned = lax.all_to_all(sending, "table", split_axis=0, concat_axis=2, tiled=True).reshape(
        columns, tables * CAP
    )
    grad_cols = jnp.zeros_like(cache).at[:, slot_ids].add(returned)
    accum_next = accum + grad_cols * grad_cols
    cache_next = cache - STEP_SIZE * grad_cols / jnp.sqrt(accum_next)
    full_grad = lax.dot_general(
        gated, live_cot, (((0,), (0,)), ((), ())), preferred_element_type=jnp.float32
    )
    by_columns = lax.psum_scatter(full_grad, "table", scatter_dimension=1, tiled=True)
    summed = lax.psum_scatter(by_columns, "replica", scatter_dimension=0, tiled=True)
    w2_step = summed / jnp.sqrt(w2_accum + summed * summed)
    return (cache_next, accum_next, w2_step)


def solution(mesh):
    return jax.shard_map(
        body,
        mesh=mesh,
        in_specs=(
            P("table", "replica"),
            P("table", "replica"),
            P("replica", None, None),
            P("replica", None),
            P("replica", None),
            P("replica", None, None, None),
            P("replica", "table", None),
            P("replica", None),
            P("replica", None),
            P("replica", "table"),
        ),
        out_specs=(P("table", "replica"), P("table", "replica"), P("replica", "table")),
        check_vma=False,
    )
```

profile of v0, /device:TPU:0, one launch (start us, length us, event | category | flops | bytes accessed | tf_op | source)
XLA Modules:
  0.0 180.1 jit_solution(12258738646778073409)
XLA Ops:
  7.2 0.7 all-gather.5.cloned.1.call-update
  7.9 1.8 %copy.119 = f32[96,4096]{0,1:T(8,128)S(1)} copy(f32[96,4096]{1,0:T(8,128)} %param.10) | data formatting | bytes 3145728 | tf_op args[0]
  9.9 0.6 gather_fusion
  10.5 2.9 %gather_fusion.1 = bf16[1024,96]{1,0:T(8,128)(2,1)S(1)} fusion(f32[96,4096]{0,1:T(8,128)S(1)} %copy.119, s32[1024]{0:T(1024)S(1)} %broadcast_clamp_fusion), kind=kCustom, calls=%fused_computation.1 | custom fusion | bytes 397312 | tf_op jit(solution)/shard_map/jit(_take)/gather | solution.py:75
  13.6 0.7 select_convert_fusion
  14.3 7.3 %all-to-all-start = ((bf16[96,8,128]{2,0,1:T(8,128)(2,1)}), bf16[96,8,128]{2,0,1:T(8,128)(2,1)S(1)}, u32[]{:S(2)}, u32[]{:S(2)}) async-start(bf16[96,8,128]{2,0,1:T(8,128)(2,1)} %select_convert_fusion), calls=%async_computation | async-start | bytes 393216 | tf_op jit(solution)/shard_map/all_to_all | solution.py:76
  21.6 0.7 all-gather.3.cloned.1.call-update
  22.5 0.6 gather_fusion.2
  23.1 0.6 dynamic_slice.6
  24.0 0.7 iota_compare_fusion.2
  24.8 0.7 fusion.48
  25.5 4.1 %all-to-all-done = bf16[96,8,128]{2,0,1:T(8,128)(2,1)S(1)} async-done(((bf16[96,8,128]{2,0,1:T(8,128)(2,1)}), bf16[96,8,128]{2,0,1:T(8,128)(2,1)S(1)}, u32[]{:S(2)}, u32[]{:S(2)}) %all-to-all-start) | async-done | bytes 196640 | tf_op jit(solution)/shard_map/all_to_all | solution.py:76
  30.1 0.5 multiply_divide_fusion
  30.6 19.1 %all-gather.5.cloned.1.call-done = bf16[768,3072]{1,0:T(8,128)(2,1)} async-done(((bf16[192,3072]{1,0:T(8,128)(2,1)}), bf16[768,3072]{1,0:T(8,128)(2,1)}) %all-gather.5.cloned.1.call-update) | async-done | bytes 4718608 | tf_op jit(solution)/shard_map/all_gather | solution.py:80
  49.7 4.4 %multiply_convert_fusion = (bf16[128,3072]{1,0:T(8,128)(2,1)S(1)}, f32[128,3072]{1,0:T(8,128)}) fusion(bf16[768,3072]{1,0:T(8,128)(2,1)} %all-gather.5.cloned.1.call-done, f32[768,128]{0,1:T(8,128)S(1)} %copy.103, f32[128]{0:T(128)S(1)} %get-tuple-element.31, f32[128]{0:T(128)S(1)} %broadcast_multiply_fusion.1), kind=kOutput, calls=%fused_computation.12 | convolution fusion | flops 606240768 | bytes 7472128 | tf_op jit(solution)/shard_map/dot_general | solution.py:81
  54.1 0.9 copy-done.2
  55.0 0.8 copy.104
  56.2 1.3 multiply_convert_fusion.1
  57.6 1.0 fusion.52
  58.7 0.7 broadcast_multiply_fusion
  59.4 0.7 fusion.22
  60.1 8.7 %all-gather.3.cloned.1.call-done = bf16[768,768]{1,0:T(8,128)(2,1)} async-done(((bf16[192,768]{1,0:T(8,128)(2,1)}), bf16[768,768]{1,0:T(8,128)(2,1)}) %all-gather.3.cloned.1.call-update) | async-done | bytes 1179664 | tf_op jit(solution)/shard_map/all_gather | solution.py:85
  68.8 1.9 %multiply_reduce_fusion = (f32[128]{0:T(128)S(1)}, f32[128,768]{1,0:T(8,128)S(1)}) fusion(f32[128,768]{1,0:T(8,128)S(1)} %copy.110, f32[128]{0:T(128)S(1)} %broadcast_multiply_fusion, bf16[128,3072]{1,0:T(8,128)(2,1)} %copy-done.2, bf16[768,768]{1,0:T(8,128)(2,1)} %all-gather.3.cloned.1.call-done, bf16[1,128,768]{2,1,0:T(8,128)(2,1)S(1)} %copy-done.3, ...), kind=kOutput, calls=%fused_computation.56 | convolution fusion | flops 151584640 | bytes 2360576 | tf_op jit(solution)/shard_map/dot_general | solution.py:83
  70.7 0.5 fusion.43
  71.3 0.6 copy-done.12
  71.8 3.0 %fusion.28 = f32[768,768]{0,1:T(8,128)} fusion(f32[128,768]{1,0:T(8,128)S(1)} %copy.110, f32[128]{0:T(128)S(1)} %broadcast_multiply_fusion, f32[128]{0:T(128)S(1)} %get-tuple-element.33, bf16[1,128,768]{2,1,0:T(8,128)(2,1)S(1)} %copy-done.3, bf16[128,3072]{1,0:T(8,128)(2,1)} %copy-done.2, bf16[128]{0:T(256)(128)(2,1)S(1)} %fusion.48), kind=kOutput, calls=%fused_computation.59 | convolution fusion | flops 151584768 | bytes 3147008 | tf_op jit(solution)/shard_map/dot_general | solution.py:104
  74.8 1.8 %fusion.50 = (f32[128]{0:T(128)S(1)}, f32[128,768]{1,0:T(8,128)S(1)}, bf16[128,768]{1,0:T(8,128)(2,1)}) fusion(f32[128]{0:T(128)} %get-tuple-element.32, f32[128,768]{1,0:T(8,128)S(1)} %copy.110, f32[128]{0:T(128)S(1)} %broadcast_multiply_fusion, f32[128]{0:T(128)} %copy-done.12, f32[128,768]{1,0:T(8,128)S(1)} %get-tuple-element.41, ...), kind=kLoop, calls=%fused_computation.111 | loop fusion | flops 1081216 | bytes 1574912 | tf_op jit(solution)/shard_map/transpose(jvp())/reduce_sum | solution.py:54
  76.9 0.7 copy-done.10
  77.6 1.8 fusion.11
  79.4 1.1 fusion.54
  80.5 1.8 copy.114
  82.2 1.8 %fusion.55 = bf16[12,128,64]{1,2,0:T(8,128)(2,1)} fusion(bf16[12,128,128]{2,1,0:T(8,128)(2,1)S(1)} %fusion.11, bf16[128,12,64]{0,2,1:T(8,128)(2,1)} %bitcast.125), kind=kOutput, calls=%fused_computation.116 | convolution fusion | flops 25165824 | bytes 786432 | tf_op jit(solution)/shard_map/transpose(jvp(sihd,sjhd->shij))/dot_general | solution.py:46
  84.1 1.7 copy.113
  85.8 1.2 fusion.53
  87.2 5.0 %fusion.25 = (f32[128]{0:T(128)S(1)}, f32[128,768]{1,0:T(8,128)S(1)}) fusion(f32[768,128]{0,1:T(8,128)S(1)} %copy.103, f32[128]{0:T(128)S(1)} %copy-done.23, f32[128]{0:T(128)S(1)} %copy-done.14, bf16[768,3072]{1,0:T(8,128)(2,1)} %all-gather.5.cloned.1.call-done, f32[128,3072]{1,0:T(8,128)} %get-tuple-element.35, bf16[128,768]{1,0:T(8,128)(2,1)} %get-tuple-element.26, ...), kind=kOutput, calls=%fused_computation.53 | convolution fusion | flops 611450752 | bytes 7865856 | tf_op jit(solution)/shard_map/dot_general | solution.py:92
  92.6 0.9 copy.115
  93.5 5.5 %all-to-all-start.1 = ((f32[8,96,128]{2,1,0:T(8,128)}), f32[8,96,128]{2,1,0:T(8,128)S(1)}, u32[]{:S(2)}, u32[]{:S(2)}) async-start(f32[8,96,128]{2,1,0:T(8,128)} %bitcast.40), calls=%async_computation.1 | async-start | bytes 786432 | tf_op jit(solution)/shard_map/all_to_all | solution.py:98
  99.1 2.8 %copy.118 = f32[96,4096]{0,1:T(8,128)} copy(f32[96,4096]{1,0:T(8,128)} %param.11) | data formatting | bytes 3145728 | tf_op args[1]
  102.0 13.1 %all-to-all-done.1 = f32[8,96,128]{2,1,0:T(8,128)S(1)} async-done(((f32[8,96,128]{2,1,0:T(8,128)}), f32[8,96,128]{2,1,0:T(8,128)S(1)}, u32[]{:S(2)}, u32[]{:S(2)}) %all-to-all-start.1) | async-done | bytes 393248 | tf_op jit(solution)/shard_map/all_to_all | solution.py:98
  115.6 7.4 %scatter_custom_fusion = f32[96,4096]{0,1:T(8,128)} fusion(s32[1024]{0:T(1024)S(1)} %bitcast.135, f32[1024,96]{1,0:T(8,128)S(1)} %copy.117, f32[]{:T(128)} %constant.61.clone.1), kind=kCustom, calls=%fused_computation.22 | custom fusion | flops 98304 | bytes 1572868 | tf_op jit(solution)/shard_map/scatter-add | solution.py:101
  123.0 26.4 %reduce-scatter.5.cloned.1.call-done = f32[768,96]{0,1:T(8,128)} async-done(((f32[768,768]{0,1:T(8,128)}), f32[768,96]{0,1:T(8,128)}) %reduce-scatter.5.cloned.1.call-update) | async-done | bytes 294928 | tf_op jit(solution)/shard_map/reduce_scatter | solution.py:107
  149.4 1.9 %copy.124 = f32[768,96]{1,0:T(8,128)} copy(f32[768,96]{0,1:T(8,128)} %reduce-scatter.5.cloned.1.call-done) | data formatting | bytes 589824
  151.3 4.6 %multiply_subtract_fusion = (f32[96,4096]{0,1:T(8,128)}, f32[96,4096]{0,1:T(8,128)}) fusion(f32[96,4096]{0,1:T(8,128)S(1)} %copy.119, f32[96,4096]{0,1:T(8,128)} %scatter_custom_fusion, f32[96,4096]{0,1:T(8,128)} %copy.118), kind=kLoop, calls=%fused_computation.5 | loop fusion | flops 1966080 | bytes 7864320 | tf_op jit(solution)/shard_map/sub | solution.py:103
  156.0 2.9 %copy.121 = f32[96,4096]{1,0:T(8,128)} copy(f32[96,4096]{0,1:T(8,128)} %get-tuple-element.20) | data formatting | bytes 3145728
  158.9 1.7 copy.122
  160.6 11.2 %reduce-scatter.7.cloned.1.call-done = f32[192,96]{1,0:T(8,128)} async-done(((f32[768,96]{1,0:T(8,128)}), f32[192,96]{1,0:T(8,128)}) %reduce-scatter.7.cloned.1.call-update) | async-done | bytes 73744
  171.8 1.0 copy.125
  172.8 0.7 copy.123
  (88 shorter events, 3.5 us)
Async XLA Ops:
  7.2 2.7 %copy-start = (s32[1,8,128]{2,1,0:T(8,128)S(1)}, s32[1,8,128]{2,1,0:T(8,128)}, u32[]{:S(2)}) copy-start(s32[1,8,128]{2,1,0:T(8,128)} %param.12) | copy-start | bytes 12292
  7.2 42.6 %all-gather.5.cloned.1.call-start = ((), (), s32[]{:S(2)}) async-start(), calls=%async_computation.5 | async-start | bytes 5898240 | tf_op jit(solution)/shard_map/all_gather | solution.py:80
  7.9 1.9 %copy-start.21 = (s32[1,8]{1,0:T(1,128)S(1)}, s32[1,8]{1,0:T(1,128)}, u32[]{:S(2)}) copy-start(s32[1,8]{1,0:T(1,128)} %param.13) | copy-start | bytes 100
  7.9 1.9 %copy-start.22 = (s32[1,8]{1,0:T(1,128)S(1)}, s32[1,8]{1,0:T(1,128)}, u32[]{:S(2)}) copy-start(s32[1,8]{1,0:T(1,128)} %param.14) | copy-start | bytes 100
  10.5 11.9 %copy-start.16 = (s32[1,8,2,2]{1,3,2,0:T(2,128)S(1)}, s32[1,8,2,2]{1,3,2,0:T(2,128)}, u32[]{:S(2)}) copy-start(s32[1,8,2,2]{1,3,2,0:T(2,128)} %param.15) | copy-start | bytes 388
  14.3 15.2 %all-to-all-start = ((bf16[96,8,128]{2,0,1:T(8,128)(2,1)}), bf16[96,8,128]{2,0,1:T(8,128)(2,1)S(1)}, u32[]{:S(2)}, u32[]{:S(2)}) async-start(bf16[96,8,128]{2,0,1:T(8,128)(2,1)} %select_convert_fusion), calls=%async_computation | async-start | bytes 393216 | tf_op jit(solution)/shard_map/all_to_all | solution.py:76
  21.6 47.2 %all-gather.3.cloned.1.call-start = ((), (), s32[]{:S(2)}) async-start(), calls=%async_computation.4 | async-start | bytes 1474560 | tf_op jit(solution)/shard_map/all_gather | solution.py:85
  22.3 127.1 %reduce-scatter.5.cloned.1.call-start = ((), (), s32[]{:S(2)}) async-start(), calls=%async_computation.6 | async-start | bytes 2654208 | tf_op jit(solution)/shard_map/reduce_scatter | solution.py:107
  29.9 24.2 %copy-start.13 = (f32[128]{0:T(128)}, f32[128]{0:T(128)S(1)}, u32[]{:S(2)}) copy-start(f32[128]{0:T(128)S(1)} %broadcast_multiply_fusion.1) | copy-start | bytes 1540
  30.1 24.0 %copy-start.19 = (f32[128]{0:T(128)}, f32[128]{0:T(128)S(1)}, u32[]{:S(2)}) copy-start(f32[128]{0:T(128)S(1)} %fusion.23) | copy-start | bytes 1540
  30.6 23.5 %copy-start.17 = (f32[128]{0:T(128)}, f32[128]{0:T(128)S(1)}, u32[]{:S(2)}) copy-start(f32[128]{0:T(128)S(1)} %get-tuple-element.31) | copy-start | bytes 1540
  54.1 0.9 copy-start.2
  56.0 1.5 copy-start.7
  56.2 1.4 copy-start.8
  56.2 1.4 copy-start.6
  57.6 1.0 copy-start.4
  57.6 11.2 %copy-start.3 = (bf16[1,128,768]{2,1,0:T(8,128)(2,1)S(1)}, bf16[1,128,768]{2,1,0:T(8,128)(2,1)}, u32[]{:S(2)}) copy-start(bf16[1,128,768]{2,1,0:T(8,128)(2,1)} %param.16) | copy-start | bytes 589828
  68.8 1.9 %copy-start.15 = (f32[128]{0:T(128)S(1)}, f32[128]{0:T(128)}, u32[]{:S(2)}) copy-start(f32[128]{0:T(128)} %fusion.22) | copy-start | bytes 1540
  71.2 0.6 copy-start.12
  76.9 0.7 copy-start.10
  77.6 1.8 %copy-start.9 = (bf16[128,768]{0,1:T(8,128)(2,1)S(1)}, bf16[128,768]{0,1:T(8,128)(2,1)}, u32[]{:S(2)}) copy-start(bf16[128,768]{0,1:T(8,128)(2,1)} %copy-done.8) | copy-start | bytes 589828
  79.4 6.4 %copy-start.5 = (bf16[12,128,128]{2,1,0:T(8,128)(2,1)S(1)}, bf16[12,128,128]{2,1,0:T(8,128)(2,1)}, u32[]{:S(2)}) copy-start(bf16[12,128,128]{2,1,0:T(8,128)(2,1)} %copy-done.4) | copy-start | bytes 1179652
  80.5 6.7 %copy-start.14 = (f32[128]{0:T(128)S(1)}, f32[128]{0:T(128)}, u32[]{:S(2)}) copy-start(f32[128]{0:T(128)} %copy-done.13) | copy-start | bytes 1540
  80.5 6.7 %copy-start.23 = (f32[128]{0:T(128)S(1)}, f32[128]{0:T(128)}, u32[]{:S(2)}) copy-start(f32[128]{0:T(128)} %get-tuple-element.30) | copy-start | bytes 1540
  87.2 5.0 %copy-start.20 = (f32[128]{0:T(128)S(1)}, f32[128]{0:T(128)}, u32[]{:S(2)}) copy-start(f32[128]{0:T(128)} %copy-done.19) | copy-start | bytes 1540
  87.2 5.0 %copy-start.18 = (f32[128]{0:T(128)S(1)}, f32[128]{0:T(128)}, u32[]{:S(2)}) copy-start(f32[128]{0:T(128)} %copy-done.17) | copy-start | bytes 1540
  93.5 21.6 %all-to-all-start.1 = ((f32[8,96,128]{2,1,0:T(8,128)}), f32[8,96,128]{2,1,0:T(8,128)S(1)}, u32[]{:S(2)}, u32[]{:S(2)}) async-start(f32[8,96,128]{2,1,0:T(8,128)} %bitcast.40), calls=%async_computation.1 | async-start | bytes 786432 | tf_op jit(solution)/shard_map/all_to_all | solution.py:98
  99.0 2.9 %copy-start.11 = (f32[192,96]{1,0:T(8,128)S(1)}, f32[192,96]{1,0:T(8,128)}, u32[]{:S(2)}) copy-start(f32[192,96]{1,0:T(8,128)} %param.19) | copy-start | bytes 221188
  99.0 72.8 %reduce-scatter.7.cloned.1.call-start = ((), (), s32[]{:S(2)}) async-start(), calls=%async_computation.7 | async-start | bytes 491520
  156.0 2.9 %copy-start.1 = (f32[96,4096]{0,1:T(8,128)S(1)}, f32[96,4096]{0,1:T(8,128)}, u32[]{:S(2)}) copy-start(f32[96,4096]{0,1:T(8,128)} %get-tuple-element.21) | copy-start | bytes 4718596
Sparse Core Ops, SparseCore 0:
  9.5 40.1 all-gather.4
  51.3 17.4 all-gather.2
  74.9 74.4 reduce-scatter.4
  151.8 20.0 reduce-scatter.6
where the time goes:
time: 181 us; the launch traced here: 180 us
  waiting for transfers between devices  84 us (46%)
  local copies, waits for them, and re-layouts  27.2 us (15%)
  matrix products  22.4 us (12%)
  other arithmetic  19.4 us (11%)
  between operations  14.2 us (8%)
  starting transfers between devices  12.9 us (7%)
    reduce_scatter x1, waiting for transfers between devices, body(): lax.psum_scatter(full_grad, 'table', scatter_dimension=1, tiled=True)  26.4 us
    all_gather x1, waiting for transfers between devices, body(): full_uqkv = lax.all_gather(w_uqkv, 'replica', axis=0, tiled=True)  19.1 us
    unnamed x57, local copies, waits for them, and re-layouts  15.3 us
    all_to_all x1, waiting for transfers between devices, body(): lax.all_to_all(sending, 'table', split_axis=0, concat_axis=2, tiled=True)  13.1 us
    unnamed x5, waiting for transfers between devices  12.6 us
    all_gather x1, waiting for transfers between devices, body(): lax.all_gather(w_out, 'replica', axis=0, tiled=True)  8.68 us
    scatter-add x1, other arithmetic, body(): grad_cols = jnp.zeros_like(cache).at[:, slot_ids].add(returned)  7.41 us
    all_to_all x1, starting transfers between devices, body(): lax.all_to_all(picked, 'table', split_axis=1, concat_axis=0, tiled=True)  7.28 us
  transfers between devices with their start and end apart: 6, of which 6 were waited for; matrix products, arithmetic and copies ran while one was open for 32% of the time, Pallas kernels for 0%

commit v1 on v0

--- a/solution.py
+++ b/solution.py
@@ -13,6 +13,14 @@
 EPS_NORM = 1e-05
 EPS_ATTN = 1e-06
 STEP_SIZE = 0.5
+
+
+def show_the_racks(payload, ndim_at):
+    payload = jnp.moveaxis(payload, 0, ndim_at)
+    view_out = payload.shape
+    return payload.reshape(
+        *view_out[:ndim_at], view_out[ndim_at] * view_out[ndim_at + 1], *view_out[ndim_at + 2 :]
+    )
 
 
 def normalize(row_data):
@@ -77,7 +85,23 @@
     embedded = arrived.reshape(D, CAP).T
     row_float = embedded.astype(jnp.float32)
     normed = normalize(row_float).astype(jnp.bfloat16)
-    full_uqkv = lax.all_gather(w_uqkv, "replica", axis=0, tiled=True)
+    devs = lax.axis_size("replica")
+    views = tuple(((d, (d + 1) % devs) for d in range(devs)))
+    queue = tuple(((b, to_i) for to_i, b in views))
+    carry_in, latest = ([], [])
+    for num in [*range(devs - 1)]:
+        if num % 2 == 0:
+            big = lax.ppermute(carry_in[-1] if carry_in else w_uqkv, "replica", views)
+            carry_in.append(big)
+        else:
+            out_arr = lax.ppermute(latest[-1] if latest else w_uqkv, "replica", queue)
+            latest.append(out_arr)
+    u_next = jnp.stack([*carry_in[::-1], w_uqkv, *latest])
+    everything = lax.axis_index("replica")
+    state_now = len(carry_in)
+    then = everything - state_now
+    u_next = u_next[(jnp.arange(devs) - then) % devs]
+    full_uqkv = show_the_racks(u_next, 0)
     hidden_pre = jnp.dot(normed, full_uqkv, preferred_element_type=jnp.float32)
     live_cot = cotangent[0] * inside.reshape(-1)[:, None].astype(jnp.bfloat16)
     d_gated = lax.dot_general(

time: 181 us -> 190 us (1.050)
  other arithmetic: 19.4 us -> 24.3 us
  local copies, waits for them, and re-layouts: 27.2 us -> 31.9 us
  waiting for transfers between devices: 84 us -> 81.7 us
    ppermute x0 -> x3, waiting for transfers between devices: none -> 28.8 us  [the longest x2 28.8 us: body(): big = lax.ppermute(carry_in[-1] if carry_in else w_uqkv, 'replica', views)]
    all_gather x1 -> x0, waiting for transfers between devices: 19.1 us -> none  [body(): full_uqkv = lax.all_gather(w_uqkv, 'replica', axis=0, tiled=True)]
    all_gather x1, waiting for transfers between devices: 8.68 us -> 0.01 us  [body(): lax.all_gather(w_out, 'replica', axis=0, tiled=True)]
    gather x0 -> x1, local copies, waits for them, and re-layouts: none -> 5.32 us  [body(): u_next = u_next[(jnp.arange(devs) - then) % devs]]
    another operation x0 -> x1, other arithmetic: none -> 4.08 us  [body(): u_next = jnp.stack([*carry_in[::-1], w_uqkv, *latest])]
    all_to_all x1, waiting for transfers between devices: 4.07 us -> 0.01 us  [body(): lax.all_to_all(picked, 'table', split_axis=1, concat_axis=0, tiled=True)]
    ppermute x0 -> x3, starting transfers between devices: none -> 2.49 us  [the longest x1 2.49 us: body(): out_arr = lax.ppermute(latest[-1] if latest else w_uqkv, 'replica', queue)]
    unnamed x5 -> x4, waiting for transfers between devices: 12.6 us -> 12.1 us
  transfers between devices with their start and end apart: 6 -> 8, of which waited for: 6 -> 5; matrix products, arithmetic and copies ran while one was open for 32% -> 36% of each run, Pallas kernels for 0% -> 0%
where the time goes in v1:
time: 190 us; the launch traced here: 189 us
  waiting for transfers between devices  81.7 us (43%)
  local copies, waits for them, and re-layouts  31.9 us (17%)
  other arithmetic  24.3 us (13%)
  matrix products  22.4 us (12%)
  starting transfers between devices  14.4 us (8%)
  between operations  14.2 us (7%)
    ppermute x2, waiting for transfers between devices, body(): big = lax.ppermute(carry_in[-1] if carry_in else w_uqkv, 'replica', views)  28.8 us
    reduce_scatter x1, waiting for transfers between devices, body(): lax.psum_scatter(full_grad, 'table', scatter_dimension=1, tiled=True)  27.5 us
    unnamed x55, local copies, waits for them, and re-layouts  15.3 us
    all_to_all x1, waiting for transfers between devices, body(): lax.all_to_all(sending, 'table', split_axis=0, concat_axis=2, tiled=True)  13.3 us
    unnamed x4, waiting for transfers between devices  12.1 us
    scatter-add x1, other arithmetic, body(): grad_cols = jnp.zeros_like(cache).at[:, slot_ids].add(returned)  7.42 us
    all_to_all x1, starting transfers between devices, body(): lax.all_to_all(sending, 'table', split_axis=0, concat_axis=2, tiled=True)  5.81 us
    all_to_all x1, starting transfers between devices, body(): lax.all_to_all(picked, 'table', split_axis=1, concat_axis=0, tiled=True)  5.81 us
  transfers between devices with their start and end apart: 8, of which 5 were waited for; matrix products, arithmetic and copies ran while one was open for 36% of the time, Pallas kernels for 0%

profile of v1, /device:TPU:0, one launch (start us, length us, event | category | flops | bytes accessed | tf_op | source)
XLA Modules:
  0.0 188.8 jit_solution(8978948444521933250)
XLA Ops:
  7.2 2.5 %collective-permute-start.2 = (bf16[192,3072]{1,0:T(8,128)(2,1)}, bf16[192,3072]{1,0:T(8,128)(2,1)}, u32[]{:S(2)}, u32[]{:S(2)}) collective-permute-start(bf16[192,3072]{1,0:T(8,128)(2,1)} %param.17), channel_id=1, source_target_pairs={{8,0},{16,8},{24,16},{0,24},{9,1},{17,9},{25,17},{1,25},{10,2},{18... | collective-permute-start | bytes 3538952 | tf_op jit(solution)/shard_map/ppermute | solution.py:97
  9.7 0.8 select_reduce_fusion
  10.4 1.8 copy.119
  12.3 0.6 gather_fusion
  12.9 2.9 %gather_fusion.1 = bf16[1024,96]{1,0:T(8,128)(2,1)S(1)} fusion(f32[96,4096]{0,1:T(8,128)S(1)} %copy.119, s32[1024]{0:T(1024)S(1)} %broadcast_clamp_fusion), kind=kCustom, calls=%fused_computation.1 | custom fusion | bytes 397312 | tf_op jit(solution)/shard_map/jit(_take)/gather | solution.py:83
  16.0 0.7 select_convert_fusion
  16.7 5.8 %all-to-all-start = ((bf16[96,8,128]{2,0,1:T(8,128)(2,1)}), bf16[96,8,128]{2,0,1:T(8,128)(2,1)S(1)}, u32[]{:S(2)}, u32[]{:S(2)}) async-start(bf16[96,8,128]{2,0,1:T(8,128)(2,1)} %select_convert_fusion), calls=%async_computation | async-start | bytes 393216 | tf_op jit(solution)/shard_map/all_to_all | solution.py:84
  22.5 0.7 all-gather.2.cloned.1.call-update
  23.3 0.6 dynamic_slice.6
  23.9 15.9 %collective-permute-done = bf16[192,3072]{1,0:T(8,128)(2,1)} collective-permute-done((bf16[192,3072]{1,0:T(8,128)(2,1)}, bf16[192,3072]{1,0:T(8,128)(2,1)}, u32[]{:S(2)}, u32[]{:S(2)}) %collective-permute-start) | collective-permute-done | bytes 1179680 | tf_op jit(solution)/shard_map/ppermute | solution.py:94
  39.8 0.7 iota_compare_fusion.2
  40.6 0.6 gather_fusion.3
  41.6 0.7 fusion.50
  43.4 12.9 %collective-permute-done.1 = bf16[192,3072]{1,0:T(8,128)(2,1)} collective-permute-done((bf16[192,3072]{1,0:T(8,128)(2,1)}, bf16[192,3072]{1,0:T(8,128)(2,1)}, u32[]{:S(2)}, u32[]{:S(2)}) %collective-permute-start.1) | collective-permute-done | bytes 1179680 | tf_op jit(solution)/shard_map/ppermute | solution.py:94
  56.3 4.1 %pad_maximum_fusion = bf16[4,192,3072]{2,1,0:T(8,128)(2,1)} fusion(bf16[1,192,3072]{2,1,0:T(8,128)(2,1)} %bitcast.18, bf16[1,192,3072]{2,1,0:T(8,128)(2,1)} %bitcast.130, bf16[1,192,3072]{2,1,0:T(8,128)(2,1)} %bitcast.16, bf16[1,192,3072]{2,1,0:T(8,128)(2,1)} %bitcast.15), kind=kLoop, calls=%fused_computation.5 | loop fusion | flops 7077888 | bytes 9437184 | tf_op jit(solution)/shard_map/stack | solution.py:99
  60.4 5.3 %gather_fusion.2 = bf16[4,192,3072]{2,1,0:T(8,128)(2,1)} fusion(bf16[4,192,3072]{2,1,0:T(8,128)(2,1)} %pad_maximum_fusion, s32[1024]{0:T(1024)S(1)} %pad_clamp_fusion), kind=kCustom, calls=%fused_computation.2 | custom fusion | bytes 9437200 | tf_op jit(solution)/shard_map/gather | solution.py:103
  65.7 4.4 %multiply_convert_fusion = (bf16[128,3072]{1,0:T(8,128)(2,1)S(1)}, f32[128,3072]{1,0:T(8,128)}) fusion(bf16[768,3072]{1,0:T(8,128)(2,1)} %bitcast.123, f32[768,128]{0,1:T(8,128)S(1)} %copy.103, f32[128]{0:T(128)S(1)} %get-tuple-element.31, f32[128]{0:T(128)S(1)} %broadcast_multiply_fusion.1), kind=kOutput, calls=%fused_computation.14 | convolution fusion | flops 606240768 | bytes 7472128 | tf_op jit(solution)/shard_map/dot_general | solution.py:105
  70.1 0.9 copy-done.2
  71.6 1.3 multiply_convert_fusion.1
  72.9 1.0 fusion.54
  74.1 0.7 broadcast_multiply_fusion
  74.7 0.7 fusion.22
  75.4 1.9 %multiply_reduce_fusion = (f32[128]{0:T(128)S(1)}, f32[128,768]{1,0:T(8,128)S(1)}) fusion(f32[128,768]{1,0:T(8,128)S(1)} %copy.110, f32[128]{0:T(128)S(1)} %broadcast_multiply_fusion, bf16[128,3072]{1,0:T(8,128)(2,1)} %copy-done.2, bf16[768,768]{1,0:T(8,128)(2,1)} %all-gather.2.cloned.1.call-done, bf16[1,128,768]{2,1,0:T(8,128)(2,1)S(1)} %copy-done.3, ...), kind=kOutput, calls=%fused_computation.58 | convolution fusion | flops 151584640 | bytes 2360576 | tf_op jit(solution)/shard_map/dot_general | solution.py:107
  77.4 0.6 fusion.45
  78.0 0.6 copy-done.13
  78.6 3.0 %fusion.28 = f32[768,768]{0,1:T(8,128)} fusion(f32[128,768]{1,0:T(8,128)S(1)} %copy.110, f32[128]{0:T(128)S(1)} %broadcast_multiply_fusion, f32[128]{0:T(128)S(1)} %get-tuple-element.33, bf16[1,128,768]{2,1,0:T(8,128)(2,1)S(1)} %copy-done.3, bf16[128,3072]{1,0:T(8,128)(2,1)} %copy-done.2, bf16[128]{0:T(256)(128)(2,1)S(1)} %fusion.50), kind=kOutput, calls=%fused_computation.61 | convolution fusion | flops 151584768 | bytes 3147008 | tf_op jit(solution)/shard_map/dot_general | solution.py:128
  81.6 1.8 fusion.52
  83.7 0.7 copy-done.10
  84.4 1.8 fusion.11
  86.2 1.1 fusion.56
  87.2 1.8 copy.114
  89.0 1.8 fusion.57
  90.8 1.8 copy.113
  92.6 1.2 fusion.55
  94.0 4.9 %fusion.25 = (f32[128]{0:T(128)S(1)}, f32[128,768]{1,0:T(8,128)S(1)}) fusion(f32[768,128]{0,1:T(8,128)S(1)} %copy.103, f32[128]{0:T(128)S(1)} %copy-done.22, f32[128]{0:T(128)S(1)} %copy-done.15, bf16[768,3072]{1,0:T(8,128)(2,1)} %bitcast.124, f32[128,3072]{1,0:T(8,128)} %get-tuple-element.35, bf16[128,768]{1,0:T(8,128)(2,1)S(1)} %copy-done.11, ...), kind=kOutput, calls=%fused_computation.55 | convolution fusion | flops 611450752 | bytes 7865856 | tf_op jit(solution)/shard_map/dot_general | solution.py:116
  99.4 0.9 copy.115
  100.3 5.8 %all-to-all-start.1 = ((f32[8,96,128]{2,1,0:T(8,128)}), f32[8,96,128]{2,1,0:T(8,128)S(1)}, u32[]{:S(2)}, u32[]{:S(2)}) async-start(f32[8,96,128]{2,1,0:T(8,128)} %bitcast.46), calls=%async_computation.1 | async-start | bytes 786432 | tf_op jit(solution)/shard_map/all_to_all | solution.py:122
  106.3 2.8 %copy.118 = f32[96,4096]{0,1:T(8,128)} copy(f32[96,4096]{1,0:T(8,128)} %param.11) | data formatting | bytes 3145728 | tf_op args[1]
  109.3 13.3 %all-to-all-done.1 = f32[8,96,128]{2,1,0:T(8,128)S(1)} async-done(((f32[8,96,128]{2,1,0:T(8,128)}), f32[8,96,128]{2,1,0:T(8,128)S(1)}, u32[]{:S(2)}, u32[]{:S(2)}) %all-to-all-start.1) | async-done | bytes 393248 | tf_op jit(solution)/shard_map/all_to_all | solution.py:122
  123.0 7.4 %scatter_custom_fusion = f32[96,4096]{0,1:T(8,128)} fusion(s32[1024]{0:T(1024)S(1)} %bitcast.145, f32[1024,96]{1,0:T(8,128)S(1)} %copy.117, f32[]{:T(128)} %constant.80.clone.1), kind=kCustom, calls=%fused_computation.24 | custom fusion | flops 98304 | bytes 1572868 | tf_op jit(solution)/shard_map/scatter-add | solution.py:125
  130.4 27.5 %reduce-scatter.5.cloned.1.call-done = f32[768,96]{0,1:T(8,128)} async-done(((f32[768,768]{0,1:T(8,128)}), f32[768,96]{0,1:T(8,128)}) %reduce-scatter.5.cloned.1.call-update) | async-done | bytes 294928 | tf_op jit(solution)/shard_map/reduce_scatter | solution.py:131
  158.0 1.9 %copy.124 = f32[768,96]{1,0:T(8,128)} copy(f32[768,96]{0,1:T(8,128)} %reduce-scatter.5.cloned.1.call-done) | data formatting | bytes 589824
  159.9 4.6 %multiply_subtract_fusion = (f32[96,4096]{0,1:T(8,128)}, f32[96,4096]{0,1:T(8,128)}) fusion(f32[96,4096]{0,1:T(8,128)S(1)} %copy.119, f32[96,4096]{0,1:T(8,128)} %scatter_custom_fusion, f32[96,4096]{0,1:T(8,128)} %copy.118), kind=kLoop, calls=%fused_computation.7 | loop fusion | flops 1966080 | bytes 7864320 | tf_op jit(solution)/shard_map/sub | solution.py:127
  164.5 2.9 %copy.121 = f32[96,4096]{1,0:T(8,128)} copy(f32[96,4096]{0,1:T(8,128)} %get-tuple-element.20) | data formatting | bytes 3145728
  167.5 1.7 copy.122
  169.2 11.4 %reduce-scatter.7.cloned.1.call-done = f32[192,96]{1,0:T(8,128)} async-done(((f32[768,96]{1,0:T(8,128)}), f32[192,96]{1,0:T(8,128)}) %reduce-scatter.7.cloned.1.call-update) | async-done | bytes 73744
  180.5 1.0 copy.125
  181.5 0.7 copy.123
  (93 shorter events, 4.3 us)
Async XLA Ops:
  7.2 5.1 %copy-start = (s32[1,8,128]{2,1,0:T(8,128)S(1)}, s32[1,8,128]{2,1,0:T(8,128)}, u32[]{:S(2)}) copy-start(s32[1,8,128]{2,1,0:T(8,128)} %param.12) | copy-start | bytes 12292
  7.2 36.2 %collective-permute-start.2 = (bf16[192,3072]{1,0:T(8,128)(2,1)}, bf16[192,3072]{1,0:T(8,128)(2,1)}, u32[]{:S(2)}, u32[]{:S(2)}) collective-permute-start(bf16[192,3072]{1,0:T(8,128)(2,1)} %param.17), channel_id=1, source_target_pairs={{8,0},{16,8},{24,16},{0,24},{9,1},{17,9},{25,17},{1,25},{10,2},{18... | collective-permute-start | bytes 3538952 | tf_op jit(solution)/shard_map/ppermute | solution.py:97
  9.7 30.1 %collective-permute-start = (bf16[192,3072]{1,0:T(8,128)(2,1)}, bf16[192,3072]{1,0:T(8,128)(2,1)}, u32[]{:S(2)}, u32[]{:S(2)}) collective-permute-start(bf16[192,3072]{1,0:T(8,128)(2,1)} %param.17), channel_id=1, source_target_pairs={{0,8},{8,16},{16,24},{24,0},{1,9},{9,17},{17,25},{25,1},{2,10},{10... | collective-permute-start | bytes 3538952 | tf_op jit(solution)/shard_map/ppermute | solution.py:94
  12.9 27.6 %copy-start.17 = (s32[1,8,2,2]{1,3,2,0:T(2,128)S(1)}, s32[1,8,2,2]{1,3,2,0:T(2,128)}, u32[]{:S(2)}) copy-start(s32[1,8,2,2]{1,3,2,0:T(2,128)} %param.15) | copy-start | bytes 388
  16.7 25.6 %all-to-all-start = ((bf16[96,8,128]{2,0,1:T(8,128)(2,1)}), bf16[96,8,128]{2,0,1:T(8,128)(2,1)S(1)}, u32[]{:S(2)}, u32[]{:S(2)}) async-start(bf16[96,8,128]{2,0,1:T(8,128)(2,1)} %select_convert_fusion), calls=%async_computation | async-start | bytes 393216 | tf_op jit(solution)/shard_map/all_to_all | solution.py:84
  22.5 52.9 %all-gather.2.cloned.1.call-start = ((), (), s32[]{:S(2)}) async-start(), calls=%async_computation.4 | async-start | bytes 1474560 | tf_op jit(solution)/shard_map/all_gather | solution.py:109
  23.2 134.7 %reduce-scatter.5.cloned.1.call-start = ((), (), s32[]{:S(2)}) async-start(), calls=%async_computation.5 | async-start | bytes 2654208 | tf_op jit(solution)/shard_map/reduce_scatter | solution.py:131
  39.8 16.5 %collective-permute-start.1 = (bf16[192,3072]{1,0:T(8,128)(2,1)}, bf16[192,3072]{1,0:T(8,128)(2,1)}, u32[]{:S(2)}, u32[]{:S(2)}) collective-permute-start(bf16[192,3072]{1,0:T(8,128)(2,1)} %collective-permute-done), channel_id=1, source_target_pairs={{0,8},{8,16},{16,24},{24,0},{1,9},{9,17},{17,25},{25,1},{2,10},{10... | collective-permute-start | bytes 3538952 | tf_op jit(solution)/shard_map/ppermute | solution.py:94
  42.7 23.1 %copy-start.14 = (f32[128]{0:T(128)}, f32[128]{0:T(128)S(1)}, u32[]{:S(2)}) copy-start(f32[128]{0:T(128)S(1)} %broadcast_multiply_fusion.1) | copy-start | bytes 1540
  42.9 17.6 %copy-start.20 = (f32[128]{0:T(128)}, f32[128]{0:T(128)S(1)}, u32[]{:S(2)}) copy-start(f32[128]{0:T(128)S(1)} %fusion.23) | copy-start | bytes 1540
  43.4 22.3 %copy-start.18 = (f32[128]{0:T(128)}, f32[128]{0:T(128)S(1)}, u32[]{:S(2)}) copy-start(f32[128]{0:T(128)S(1)} %get-tuple-element.31) | copy-start | bytes 1540
  70.1 0.9 copy-start.2
  71.2 1.7 copy-start.6
  71.4 1.5 copy-start.7
  71.5 1.3 copy-start.8
  72.9 1.0 copy-start.4
  72.9 2.5 %copy-start.3 = (bf16[1,128,768]{2,1,0:T(8,128)(2,1)S(1)}, bf16[1,128,768]{2,1,0:T(8,128)(2,1)}, u32[]{:S(2)}) copy-start(bf16[1,128,768]{2,1,0:T(8,128)(2,1)} %param.16) | copy-start | bytes 589828
  75.4 1.9 %copy-start.16 = (f32[128]{0:T(128)S(1)}, f32[128]{0:T(128)}, u32[]{:S(2)}) copy-start(f32[128]{0:T(128)} %fusion.22) | copy-start | bytes 1540
  78.0 0.6 copy-start.13
  83.7 0.7 copy-start.10
  84.4 1.8 copy-start.9
  86.2 6.5 %copy-start.5 = (bf16[12,128,128]{2,1,0:T(8,128)(2,1)S(1)}, bf16[12,128,128]{2,1,0:T(8,128)(2,1)}, u32[]{:S(2)}) copy-start(bf16[12,128,128]{2,1,0:T(8,128)(2,1)} %copy-done.4) | copy-start | bytes 1179652
  87.2 6.7 %copy-start.15 = (f32[128]{0:T(128)S(1)}, f32[128]{0:T(128)}, u32[]{:S(2)}) copy-start(f32[128]{0:T(128)} %copy-done.14) | copy-start | bytes 1540
  87.2 6.7 %copy-start.22 = (f32[128]{0:T(128)S(1)}, f32[128]{0:T(128)}, u32[]{:S(2)}) copy-start(f32[128]{0:T(128)} %get-tuple-element.30) | copy-start | bytes 1540
  90.8 3.1 %copy-start.11 = (bf16[128,768]{1,0:T(8,128)(2,1)S(1)}, bf16[128,768]{1,0:T(8,128)(2,1)}, u32[]{:S(2)}) copy-start(bf16[128,768]{1,0:T(8,128)(2,1)} %get-tuple-element.26) | copy-start | bytes 589828
  94.0 5.0 %copy-start.21 = (f32[128]{0:T(128)S(1)}, f32[128]{0:T(128)}, u32[]{:S(2)}) copy-start(f32[128]{0:T(128)} %copy-done.20) | copy-start | bytes 1540
  94.0 5.0 %copy-start.19 = (f32[128]{0:T(128)S(1)}, f32[128]{0:T(128)}, u32[]{:S(2)}) copy-start(f32[128]{0:T(128)} %copy-done.18) | copy-start | bytes 1540
  100.3 22.2 %all-to-all-start.1 = ((f32[8,96,128]{2,1,0:T(8,128)}), f32[8,96,128]{2,1,0:T(8,128)S(1)}, u32[]{:S(2)}, u32[]{:S(2)}) async-start(f32[8,96,128]{2,1,0:T(8,128)} %bitcast.46), calls=%async_computation.1 | async-start | bytes 786432 | tf_op jit(solution)/shard_map/all_to_all | solution.py:122
  106.1 3.1 %copy-start.12 = (f32[192,96]{1,0:T(8,128)S(1)}, f32[192,96]{1,0:T(8,128)}, u32[]{:S(2)}) copy-start(f32[192,96]{1,0:T(8,128)} %param.19) | copy-start | bytes 221188
  106.1 74.4 %reduce-scatter.7.cloned.1.call-start = ((), (), s32[]{:S(2)}) async-start(), calls=%async_computation.6 | async-start | bytes 491520
  164.5 2.9 %copy-start.1 = (f32[96,4096]{0,1:T(8,128)S(1)}, f32[96,4096]{0,1:T(8,128)}, u32[]{:S(2)}) copy-start(f32[96,4096]{0,1:T(8,128)} %get-tuple-element.21) | copy-start | bytes 4718596
Sparse Core Ops, SparseCore 0:
  24.9 20.4 all-gather.1
  81.7 76.2 reduce-scatter.4
  160.5 20.0 reduce-scatter.6
